TPU v7x, 32 devices: a whole 2x2x4 slice. The times are simulated.
32 devices in a mesh: sec: 8 (over y, x, core), ch: 4 (over z).
Axes of the slice: x: 2, y: 2, z: 4, core: 2. Of those that a mesh axis runs over, the one named last changes fastest.
Arguments:
- start_amps: bfloat16 [6, 1024, 2048], P(None, 'ch'), may hold values from -6 to 6
- energies: float32 [6], replicated, may hold values from 0.5 to 2
- thresholds: bfloat16 [8, 1024], P('sec', 'ch'), may hold values from -3 to -1
- intersection: bfloat16 [8, 1024, 1024], P('sec', 'ch'), may hold values from -0.2 to 1
Outputs:
- boundary_amps: bfloat16 [8, 6, 1024, 2048], P('sec', None, 'ch')
All inputs are finite; a program needn't handle non-finite values.
Results may differ from a plain program's by a relative error of at most 0.04.
Values may be sent and summed in bfloat16 or wider, within the bound.
A program may use at most 64 MiB of HBM per device.

v0:
```python
import jax
import jax.numpy as jnp
from jax import lax
from jax.sharding import PartitionSpec as P


def passed_along(value, axis, steps):
    count = lax.axis_size(axis)
    leading, last = (max(0, -steps), min(count, count - steps))
    return lax.ppermute(value, axis, [(source, source + steps) for source in range(leading, last)])


def per_device(start_amps, energies, thresholds, intersection):
    sectors = lax.axis_size("sec")
    sector_index = lax.axis_index("sec")
    groups = lax.axis_size("ch")
    energy_count = energies.shape[0]
    step_count = sectors + energy_count - 1
    row_count = intersection.shape[1]
    width_cols = start_amps.shape[2]
    half_cols = width_cols // 2
    col_width = half_cols // groups
    intersection_whole, thresholds_whole = (
        lax.all_gather(intersection, "ch", axis=1, tiled=True),
        lax.all_gather(thresholds, "ch", axis=1, tiled=True),
    )
    basis_change = intersection_whole[0]
    channel_thresholds = thresholds_whole[0].astype(jnp.float32)
    channel_count = basis_change.shape[0]
    paired = start_amps.reshape(energy_count, row_count, 2, half_cols)
    start_cols = lax.all_to_all(paired, "ch", split_axis=3, concat_axis=1, tiled=True)
    stored_init = jnp.zeros((energy_count, channel_count, 2, col_width), jnp.bfloat16)

    def multiply(flat):
        return jnp.dot(basis_change, flat, preferred_element_type=jnp.float32).astype(jnp.bfloat16)

    def skipped(flat):
        return jnp.zeros((channel_count, 2 * col_width), jnp.bfloat16)

    def step(step_index, state_pair):
        outgoing, stored = state_pair
        incoming = passed_along(outgoing, "sec", 1)
        energy_raw = step_index - sector_index
        active = (energy_raw >= 0) & (energy_raw < energy_count)
        energy_slot = jnp.clip(energy_raw, 0, energy_count - 1)
        initial = lax.dynamic_index_in_dim(start_cols, energy_slot, 0, keepdims=False)
        source = jnp.where(sector_index == 0, initial, incoming).astype(jnp.float32)
        wavenumber = jnp.sqrt(energies[energy_slot] - channel_thresholds)[:, None]
        values_part = source[:, 0, :]
        slopes_part = source[:, 1, :]
        cosine = jnp.cos(wavenumber)
        sine_term = jnp.sin(wavenumber)
        new_values = cosine * values_part + sine_term / wavenumber * slopes_part
        new_slopes = -wavenumber * sine_term * values_part + cosine * slopes_part
        rotated = jnp.stack([new_values, new_slopes], axis=1).astype(jnp.bfloat16)
        flat = rotated.reshape(channel_count, 2 * col_width)
        fresh = lax.cond(active, multiply, skipped, flat)
        fresh = fresh.reshape(channel_count, 2, col_width)
        previous = lax.dynamic_index_in_dim(stored, energy_slot, 0, keepdims=False)
        kept = jnp.where(active, fresh, previous)
        stored = lax.dynamic_update_index_in_dim(stored, kept, energy_slot, 0)
        return (fresh, stored)

    outgoing_init = jnp.zeros((channel_count, 2, col_width), jnp.bfloat16)
    final_pair = lax.fori_loop(0, step_count, step, (outgoing_init, stored_init))
    returned = lax.all_to_all(final_pair[1], "ch", split_axis=1, concat_axis=3, tiled=True)
    return returned.reshape(energy_count, row_count, width_cols)[None]


def solution(mesh):
    in_specs = (P(None, "ch", None), P(), P("sec", "ch"), P("sec", "ch", None))
    out_specs = P("sec", None, "ch", None)
    return jax.shard_map(
        per_device, mesh=mesh, in_specs=in_specs, out_specs=out_specs, check_vma=False
    )
```

profile of v0, /device:TPU:7, one launch (start us, length us, event | category | flops | bytes accessed | tf_op | source)
XLA Modules:
  0.0 733.0 jit_solution(3226323656198132357)
XLA Ops:
  6.5 8.6 %copy.31 = bf16[6,256,2048]{1,2,0:T(8,128)(2,1)} copy(bf16[6,256,2048]{2,1,0:T(8,128)(2,1)} %param.8) | data formatting | bytes 12582912 | tf_op args[0]
  15.1 12.7 %copy.32 = bf16[6,256,2,1024]{1,2,0,3:T(2,128)(2,1)} copy(bf16[6,256,2,1024]{1,3,2,0:T(8,128)(2,1)} %bitcast.29) | data formatting | bytes 12582912 | tf_op jit(solution)/shard_map/reshape | solution.py:30
  27.9 5.4 all-to-all-start
  34.0 138.7 %all_gather.6 = bf16[1,1024]{1,0:T(2,128)(2,1)S(1)} all-gather(bf16[1,256]{1,0:T(2,128)(2,1)S(1)} %copy-done), channel_id=1, replica_groups=mesh['sec'=8,'ch'=4] {'ch'}, dimensions={1}, use_global_device_ids=true | all-gather | bytes 2560 | tf_op jit(solution)/shard_map/all_gather | solution.py:25
  172.7 31.9 %all-to-all-done = bf16[6,256,2,1024]{1,2,0,3:T(2,128)(2,1)} async-done(((bf16[6,256,2,1024]{1,2,0,3:T(2,128)(2,1)}), bf16[6,256,2,1024]{1,2,0,3:T(2,128)(2,1)}, u32[]{:S(2)}, u32[]{:S(2)}) %all-to-all-start) | async-done | bytes 6291488 | tf_op jit(solution)/shard_map/all_to_all | solution.py:31
  204.6 6.4 copy.33
  211.1 8.6 %copy.34 = bf16[6,4,256,2,256]{4,2,1,3,0:T(8,128)(2,1)} copy(bf16[6,4,256,2,256]{2,4,1,3,0:T(8,128)(2,1)} %bitcast.27) | data formatting | bytes 12582912 | tf_op jit(solution)/shard_map/all_to_all | solution.py:31
  220.8 5.9 broadcast_in_dim.14.clone
  226.8 337.5 %while.16 = (s32[]{:T(128)}, bf16[1024,2,256]{0,2,1:T(8,128)(2,1)}, bf16[6,1024,2,256]{3,2,0,1:T(2,128)(2,1)}, s32[]{:T(128)}, f32[6]{0:T(128)S(1)}, /*index=5*/...) while((s32[]{:T(128)}, bf16[1024,2,256]{0,2,1:T(8,128)(2,1)}, ...), condition=%wide.region_3.4_spmd, body=%wide.region_0.3_spmd.sunk | while | flops 1078464512 | bytes 46166332 | solution.py:65
  249.8 9.5 %collective-permute-done = bf16[1024,2,256]{2,0,1:T(8,128)(2,1)S(1)} collective-permute-done((bf16[1024,2,256]{2,0,1:T(8,128)(2,1)}, bf16[1024,2,256]{2,0,1:T(8,128)(2,1)S(1)}, u32[]{:S(2)}, u32[]{:S(2)}) %collective-permute-start) | collective-permute-done | bytes 1048608 | tf_op jit(solution)/shard_map/while/body/eval_jaxpr/ppermute | solution.py:10
  273.8 10.0 %collective-permute-done = bf16[1024,2,256]{2,0,1:T(8,128)(2,1)S(1)} collective-permute-done((bf16[1024,2,256]{2,0,1:T(8,128)(2,1)}, bf16[1024,2,256]{2,0,1:T(8,128)(2,1)S(1)}, u32[]{:S(2)}, u32[]{:S(2)}) %collective-permute-start) | collective-permute-done | bytes 1048608 | tf_op jit(solution)/shard_map/while/body/eval_jaxpr/ppermute | solution.py:10
  298.4 10.0 %collective-permute-done = bf16[1024,2,256]{2,0,1:T(8,128)(2,1)S(1)} collective-permute-done((bf16[1024,2,256]{2,0,1:T(8,128)(2,1)}, bf16[1024,2,256]{2,0,1:T(8,128)(2,1)S(1)}, u32[]{:S(2)}, u32[]{:S(2)}) %collective-permute-start) | collective-permute-done | bytes 1048608 | tf_op jit(solution)/shard_map/while/body/eval_jaxpr/ppermute | solution.py:10
  323.0 10.0 %collective-permute-done = bf16[1024,2,256]{2,0,1:T(8,128)(2,1)S(1)} collective-permute-done((bf16[1024,2,256]{2,0,1:T(8,128)(2,1)}, bf16[1024,2,256]{2,0,1:T(8,128)(2,1)S(1)}, u32[]{:S(2)}, u32[]{:S(2)}) %collective-permute-start) | collective-permute-done | bytes 1048608 | tf_op jit(solution)/shard_map/while/body/eval_jaxpr/ppermute | solution.py:10
  347.5 10.0 %collective-permute-done = bf16[1024,2,256]{2,0,1:T(8,128)(2,1)S(1)} collective-permute-done((bf16[1024,2,256]{2,0,1:T(8,128)(2,1)}, bf16[1024,2,256]{2,0,1:T(8,128)(2,1)S(1)}, u32[]{:S(2)}, u32[]{:S(2)}) %collective-permute-start) | collective-permute-done | bytes 1048608 | tf_op jit(solution)/shard_map/while/body/eval_jaxpr/ppermute | solution.py:10
  372.1 10.0 %collective-permute-done = bf16[1024,2,256]{2,0,1:T(8,128)(2,1)S(1)} collective-permute-done((bf16[1024,2,256]{2,0,1:T(8,128)(2,1)}, bf16[1024,2,256]{2,0,1:T(8,128)(2,1)S(1)}, u32[]{:S(2)}, u32[]{:S(2)}) %collective-permute-start) | collective-permute-done | bytes 1048608 | tf_op jit(solution)/shard_map/while/body/eval_jaxpr/ppermute | solution.py:10
  396.7 14.9 %collective-permute-done = bf16[1024,2,256]{2,0,1:T(8,128)(2,1)S(1)} collective-permute-done((bf16[1024,2,256]{2,0,1:T(8,128)(2,1)}, bf16[1024,2,256]{2,0,1:T(8,128)(2,1)S(1)}, u32[]{:S(2)}, u32[]{:S(2)}) %collective-permute-start) | collective-permute-done | bytes 1048608 | tf_op jit(solution)/shard_map/while/body/eval_jaxpr/ppermute | solution.py:10
  413.5 4.9 conditional.2
  429.7 10.0 %collective-permute-done = bf16[1024,2,256]{2,0,1:T(8,128)(2,1)S(1)} collective-permute-done((bf16[1024,2,256]{2,0,1:T(8,128)(2,1)}, bf16[1024,2,256]{2,0,1:T(8,128)(2,1)S(1)}, u32[]{:S(2)}, u32[]{:S(2)}) %collective-permute-start) | collective-permute-done | bytes 1048608 | tf_op jit(solution)/shard_map/while/body/eval_jaxpr/ppermute | solution.py:10
  441.7 4.9 conditional.2
  457.9 10.0 %collective-permute-done = bf16[1024,2,256]{2,0,1:T(8,128)(2,1)S(1)} collective-permute-done((bf16[1024,2,256]{2,0,1:T(8,128)(2,1)}, bf16[1024,2,256]{2,0,1:T(8,128)(2,1)S(1)}, u32[]{:S(2)}, u32[]{:S(2)}) %collective-permute-start) | collective-permute-done | bytes 1048608 | tf_op jit(solution)/shard_map/while/body/eval_jaxpr/ppermute | solution.py:10
  469.9 4.9 conditional.2
  486.1 10.4 %collective-permute-done = bf16[1024,2,256]{2,0,1:T(8,128)(2,1)S(1)} collective-permute-done((bf16[1024,2,256]{2,0,1:T(8,128)(2,1)}, bf16[1024,2,256]{2,0,1:T(8,128)(2,1)S(1)}, u32[]{:S(2)}, u32[]{:S(2)}) %collective-permute-start) | collective-permute-done | bytes 1048608 | tf_op jit(solution)/shard_map/while/body/eval_jaxpr/ppermute | solution.py:10
  498.4 4.9 conditional.2
  499.8 2.3 convolution_convert_fusion
  514.6 10.9 %collective-permute-done = bf16[1024,2,256]{2,0,1:T(8,128)(2,1)S(1)} collective-permute-done((bf16[1024,2,256]{2,0,1:T(8,128)(2,1)}, bf16[1024,2,256]{2,0,1:T(8,128)(2,1)S(1)}, u32[]{:S(2)}, u32[]{:S(2)}) %collective-permute-start) | collective-permute-done | bytes 1048608 | tf_op jit(solution)/shard_map/while/body/eval_jaxpr/ppermute | solution.py:10
  527.5 4.9 conditional.2
  528.9 2.3 convolution_convert_fusion
  543.7 10.9 %collective-permute-done = bf16[1024,2,256]{2,0,1:T(8,128)(2,1)S(1)} collective-permute-done((bf16[1024,2,256]{2,0,1:T(8,128)(2,1)}, bf16[1024,2,256]{2,0,1:T(8,128)(2,1)S(1)}, u32[]{:S(2)}, u32[]{:S(2)}) %collective-permute-start) | collective-permute-done | bytes 1048608 | tf_op jit(solution)/shard_map/while/body/eval_jaxpr/ppermute | solution.py:10
  556.6 4.9 conditional.2
  564.3 140.1 %all_to_all.33 = bf16[6,1024,2,256]{3,2,0,1:T(2,128)(2,1)S(1)} all-to-all(bf16[6,1024,2,256]{3,2,0,1:T(2,128)(2,1)} %get-tuple-element.205), channel_id=1, replica_groups=mesh['sec'=8,'ch'=4] {'ch'}, dimensions={1} | all-to-all | bytes 12582912 | tf_op jit(solution)/shard_map/all_to_all | solution.py:66
  704.4 10.7 %copy.36 = bf16[6,256,2,4,256]{4,3,2,1,0:T(4,128)(2,1)} copy(bf16[6,256,2,4,256]{4,2,0,1,3:T(2,128)(2,1)S(1)} %bitcast.28) | data formatting | bytes 12582912 | tf_op jit(solution)/shard_map/all_to_all | solution.py:66
  715.1 11.0 %broadcast_in_dim_reshape.3 = bf16[1,6,256,2048]{3,2,1,0:T(8,128)(2,1)} reshape(bf16[6,256,2,4,256]{4,3,2,1,0:T(4,128)(2,1)} %copy.36) | data formatting | bytes 12582912 | tf_op jit(solution)/shard_map/broadcast_in_dim;reshape | solution.py:67
  (235 shorter events, 215.2 us)
Async XLA Ops:
  27.9 6.1 copy-start
  27.9 176.8 %all-to-all-start = ((bf16[6,256,2,1024]{1,2,0,3:T(2,128)(2,1)}), bf16[6,256,2,1024]{1,2,0,3:T(2,128)(2,1)}, u32[]{:S(2)}, u32[]{:S(2)}) async-start(bf16[6,256,2,1024]{1,2,0,3:T(2,128)(2,1)} %copy.32), calls=%async_computation | async-start | bytes 12582912 | tf_op jit(solution)/shard_map/all_to_all | solution.py:31
  33.3 186.4 %all-gather.2.cloned.1.call-start = ((), (), s32[]{:S(2)}) async-start(), calls=%async_computation.2 | async-start | bytes 2621440 | tf_op jit(solution)/shard_map/all_gather | solution.py:24
  219.7 7.1 copy-start.2
  229.0 6.3 collective-permute-start
  234.4 2.9 copy-start.1
  243.6 15.8 %collective-permute-start = (bf16[1024,2,256]{2,0,1:T(8,128)(2,1)}, bf16[1024,2,256]{2,0,1:T(8,128)(2,1)S(1)}, u32[]{:S(2)}, u32[]{:S(2)}) collective-permute-start(bf16[1024,2,256]{2,0,1:T(8,128)(2,1)} %copy.45), channel_id=1, source_target_pairs={{0,4},{4,8},{8,12},{12,16},{16,20},{20,24},{24,28},{1,5},{5,9},{9,... | collective-permute-start | bytes 3145736 | tf_op jit(solution)/shard_map/while/body/eval_jaxpr/ppermute | solution.py:10
  248.9 12.3 %copy-start.1 = (bf16[1024,1024]{1,0:T(8,128)(2,1)S(1)}, bf16[1024,1024]{1,0:T(8,128)(2,1)}, u32[]{:S(2)}) copy-start(bf16[1024,1024]{1,0:T(8,128)(2,1)} %get-tuple-element.365) | copy-start | bytes 6291460 | tf_op jit(solution)/shard_map/while
  267.6 16.3 %collective-permute-start = (bf16[1024,2,256]{2,0,1:T(8,128)(2,1)}, bf16[1024,2,256]{2,0,1:T(8,128)(2,1)S(1)}, u32[]{:S(2)}, u32[]{:S(2)}) collective-permute-start(bf16[1024,2,256]{2,0,1:T(8,128)(2,1)} %copy.45), channel_id=1, source_target_pairs={{0,4},{4,8},{8,12},{12,16},{16,20},{20,24},{24,28},{1,5},{5,9},{9,... | collective-permute-start | bytes 3145736 | tf_op jit(solution)/shard_map/while/body/eval_jaxpr/ppermute | solution.py:10
  272.9 12.9 %copy-start.1 = (bf16[1024,1024]{1,0:T(8,128)(2,1)S(1)}, bf16[1024,1024]{1,0:T(8,128)(2,1)}, u32[]{:S(2)}) copy-start(bf16[1024,1024]{1,0:T(8,128)(2,1)} %get-tuple-element.365) | copy-start | bytes 6291460 | tf_op jit(solution)/shard_map/while
  292.1 16.3 %collective-permute-start = (bf16[1024,2,256]{2,0,1:T(8,128)(2,1)}, bf16[1024,2,256]{2,0,1:T(8,128)(2,1)S(1)}, u32[]{:S(2)}, u32[]{:S(2)}) collective-permute-start(bf16[1024,2,256]{2,0,1:T(8,128)(2,1)} %copy.45), channel_id=1, source_target_pairs={{0,4},{4,8},{8,12},{12,16},{16,20},{20,24},{24,28},{1,5},{5,9},{9,... | collective-permute-start | bytes 3145736 | tf_op jit(solution)/shard_map/while/body/eval_jaxpr/ppermute | solution.py:10
  297.5 12.9 %copy-start.1 = (bf16[1024,1024]{1,0:T(8,128)(2,1)S(1)}, bf16[1024,1024]{1,0:T(8,128)(2,1)}, u32[]{:S(2)}) copy-start(bf16[1024,1024]{1,0:T(8,128)(2,1)} %get-tuple-element.365) | copy-start | bytes 6291460 | tf_op jit(solution)/shard_map/while
  316.7 16.3 %collective-permute-start = (bf16[1024,2,256]{2,0,1:T(8,128)(2,1)}, bf16[1024,2,256]{2,0,1:T(8,128)(2,1)S(1)}, u32[]{:S(2)}, u32[]{:S(2)}) collective-permute-start(bf16[1024,2,256]{2,0,1:T(8,128)(2,1)} %copy.45), channel_id=1, source_target_pairs={{0,4},{4,8},{8,12},{12,16},{16,20},{20,24},{24,28},{1,5},{5,9},{9,... | collective-permute-start | bytes 3145736 | tf_op jit(solution)/shard_map/while/body/eval_jaxpr/ppermute | solution.py:10
  322.1 12.9 %copy-start.1 = (bf16[1024,1024]{1,0:T(8,128)(2,1)S(1)}, bf16[1024,1024]{1,0:T(8,128)(2,1)}, u32[]{:S(2)}) copy-start(bf16[1024,1024]{1,0:T(8,128)(2,1)} %get-tuple-element.365) | copy-start | bytes 6291460 | tf_op jit(solution)/shard_map/while
  341.3 16.3 %collective-permute-start = (bf16[1024,2,256]{2,0,1:T(8,128)(2,1)}, bf16[1024,2,256]{2,0,1:T(8,128)(2,1)S(1)}, u32[]{:S(2)}, u32[]{:S(2)}) collective-permute-start(bf16[1024,2,256]{2,0,1:T(8,128)(2,1)} %copy.45), channel_id=1, source_target_pairs={{0,4},{4,8},{8,12},{12,16},{16,20},{20,24},{24,28},{1,5},{5,9},{9,... | collective-permute-start | bytes 3145736 | tf_op jit(solution)/shard_map/while/body/eval_jaxpr/ppermute | solution.py:10
  346.6 12.9 %copy-start.1 = (bf16[1024,1024]{1,0:T(8,128)(2,1)S(1)}, bf16[1024,1024]{1,0:T(8,128)(2,1)}, u32[]{:S(2)}) copy-start(bf16[1024,1024]{1,0:T(8,128)(2,1)} %get-tuple-element.365) | copy-start | bytes 6291460 | tf_op jit(solution)/shard_map/while
  365.8 16.3 %collective-permute-start = (bf16[1024,2,256]{2,0,1:T(8,128)(2,1)}, bf16[1024,2,256]{2,0,1:T(8,128)(2,1)S(1)}, u32[]{:S(2)}, u32[]{:S(2)}) collective-permute-start(bf16[1024,2,256]{2,0,1:T(8,128)(2,1)} %copy.45), channel_id=1, source_target_pairs={{0,4},{4,8},{8,12},{12,16},{16,20},{20,24},{24,28},{1,5},{5,9},{9,... | collective-permute-start | bytes 3145736 | tf_op jit(solution)/shard_map/while/body/eval_jaxpr/ppermute | solution.py:10
  371.2 12.9 %copy-start.1 = (bf16[1024,1024]{1,0:T(8,128)(2,1)S(1)}, bf16[1024,1024]{1,0:T(8,128)(2,1)}, u32[]{:S(2)}) copy-start(bf16[1024,1024]{1,0:T(8,128)(2,1)} %get-tuple-element.365) | copy-start | bytes 6291460 | tf_op jit(solution)/shard_map/while
  390.4 21.2 %collective-permute-start = (bf16[1024,2,256]{2,0,1:T(8,128)(2,1)}, bf16[1024,2,256]{2,0,1:T(8,128)(2,1)S(1)}, u32[]{:S(2)}, u32[]{:S(2)}) collective-permute-start(bf16[1024,2,256]{2,0,1:T(8,128)(2,1)} %copy.45), channel_id=1, source_target_pairs={{0,4},{4,8},{8,12},{12,16},{16,20},{20,24},{24,28},{1,5},{5,9},{9,... | collective-permute-start | bytes 3145736 | tf_op jit(solution)/shard_map/while/body/eval_jaxpr/ppermute | solution.py:10
  395.8 17.7 %copy-start.1 = (bf16[1024,1024]{1,0:T(8,128)(2,1)S(1)}, bf16[1024,1024]{1,0:T(8,128)(2,1)}, u32[]{:S(2)}) copy-start(bf16[1024,1024]{1,0:T(8,128)(2,1)} %get-tuple-element.365) | copy-start | bytes 6291460 | tf_op jit(solution)/shard_map/while
  423.4 16.3 %collective-permute-start = (bf16[1024,2,256]{2,0,1:T(8,128)(2,1)}, bf16[1024,2,256]{2,0,1:T(8,128)(2,1)S(1)}, u32[]{:S(2)}, u32[]{:S(2)}) collective-permute-start(bf16[1024,2,256]{2,0,1:T(8,128)(2,1)} %copy.45), channel_id=1, source_target_pairs={{0,4},{4,8},{8,12},{12,16},{16,20},{20,24},{24,28},{1,5},{5,9},{9,... | collective-permute-start | bytes 3145736 | tf_op jit(solution)/shard_map/while/body/eval_jaxpr/ppermute | solution.py:10
  428.8 12.9 %copy-start.1 = (bf16[1024,1024]{1,0:T(8,128)(2,1)S(1)}, bf16[1024,1024]{1,0:T(8,128)(2,1)}, u32[]{:S(2)}) copy-start(bf16[1024,1024]{1,0:T(8,128)(2,1)} %get-tuple-element.365) | copy-start | bytes 6291460 | tf_op jit(solution)/shard_map/while
  451.6 16.3 %collective-permute-start = (bf16[1024,2,256]{2,0,1:T(8,128)(2,1)}, bf16[1024,2,256]{2,0,1:T(8,128)(2,1)S(1)}, u32[]{:S(2)}, u32[]{:S(2)}) collective-permute-start(bf16[1024,2,256]{2,0,1:T(8,128)(2,1)} %copy.45), channel_id=1, source_target_pairs={{0,4},{4,8},{8,12},{12,16},{16,20},{20,24},{24,28},{1,5},{5,9},{9,... | collective-permute-start | bytes 3145736 | tf_op jit(solution)/shard_map/while/body/eval_jaxpr/ppermute | solution.py:10
  457.0 12.9 %copy-start.1 = (bf16[1024,1024]{1,0:T(8,128)(2,1)S(1)}, bf16[1024,1024]{1,0:T(8,128)(2,1)}, u32[]{:S(2)}) copy-start(bf16[1024,1024]{1,0:T(8,128)(2,1)} %get-tuple-element.365) | copy-start | bytes 6291460 | tf_op jit(solution)/shard_map/while
  479.8 16.7 %collective-permute-start = (bf16[1024,2,256]{2,0,1:T(8,128)(2,1)}, bf16[1024,2,256]{2,0,1:T(8,128)(2,1)S(1)}, u32[]{:S(2)}, u32[]{:S(2)}) collective-permute-start(bf16[1024,2,256]{2,0,1:T(8,128)(2,1)} %copy.45), channel_id=1, source_target_pairs={{0,4},{4,8},{8,12},{12,16},{16,20},{20,24},{24,28},{1,5},{5,9},{9,... | collective-permute-start | bytes 3145736 | tf_op jit(solution)/shard_map/while/body/eval_jaxpr/ppermute | solution.py:10
  485.2 13.3 %copy-start.1 = (bf16[1024,1024]{1,0:T(8,128)(2,1)S(1)}, bf16[1024,1024]{1,0:T(8,128)(2,1)}, u32[]{:S(2)}) copy-start(bf16[1024,1024]{1,0:T(8,128)(2,1)} %get-tuple-element.365) | copy-start | bytes 6291460 | tf_op jit(solution)/shard_map/while
  508.3 17.2 %collective-permute-start = (bf16[1024,2,256]{2,0,1:T(8,128)(2,1)}, bf16[1024,2,256]{2,0,1:T(8,128)(2,1)S(1)}, u32[]{:S(2)}, u32[]{:S(2)}) collective-permute-start(bf16[1024,2,256]{2,0,1:T(8,128)(2,1)} %copy.45), channel_id=1, source_target_pairs={{0,4},{4,8},{8,12},{12,16},{16,20},{20,24},{24,28},{1,5},{5,9},{9,... | collective-permute-start | bytes 3145736 | tf_op jit(solution)/shard_map/while/body/eval_jaxpr/ppermute | solution.py:10
  513.7 13.8 %copy-start.1 = (bf16[1024,1024]{1,0:T(8,128)(2,1)S(1)}, bf16[1024,1024]{1,0:T(8,128)(2,1)}, u32[]{:S(2)}) copy-start(bf16[1024,1024]{1,0:T(8,128)(2,1)} %get-tuple-element.365) | copy-start | bytes 6291460 | tf_op jit(solution)/shard_map/while
  537.4 17.2 %collective-permute-start = (bf16[1024,2,256]{2,0,1:T(8,128)(2,1)}, bf16[1024,2,256]{2,0,1:T(8,128)(2,1)S(1)}, u32[]{:S(2)}, u32[]{:S(2)}) collective-permute-start(bf16[1024,2,256]{2,0,1:T(8,128)(2,1)} %copy.45), channel_id=1, source_target_pairs={{0,4},{4,8},{8,12},{12,16},{16,20},{20,24},{24,28},{1,5},{5,9},{9,... | collective-permute-start | bytes 3145736 | tf_op jit(solution)/shard_map/while/body/eval_jaxpr/ppermute | solution.py:10
  542.8 13.8 %copy-start.1 = (bf16[1024,1024]{1,0:T(8,128)(2,1)S(1)}, bf16[1024,1024]{1,0:T(8,128)(2,1)}, u32[]{:S(2)}) copy-start(bf16[1024,1024]{1,0:T(8,128)(2,1)} %get-tuple-element.365) | copy-start | bytes 6291460 | tf_op jit(solution)/shard_map/while
Sparse Core Ops, SparseCore 0:
  35.6 86.9 all-gather.1
where the time goes:
time: 746 us; the launch traced here: 733 us
  blocking collectives  279 us (37%)
  local copies, waits for them, and re-layouts  206 us (28%)
  waiting for transfers between devices  160 us (21%)
  other arithmetic  38.1 us (5%)
  starting transfers between devices  22.1 us (3%)
  matrix products  13.9 us (2%)
  between operations  13.4 us (2%)
    all_to_all x1, blocking collectives, per_device(): lax.all_to_all(final_pair[1], 'ch', split_axis=1, concat_axis=3, tiled=True)  140 us
    all_gather x1, blocking collectives, per_device(): lax.all_gather(thresholds, 'ch', axis=1, tiled=True)  139 us
    ppermute x13, waiting for transfers between devices, passed_along(): lax.ppermute(value, axis, [(source, source + steps) for source in range(l...  127 us
    dynamic_slice x26, local copies, waits for them, and re-layouts, step(): previous = lax.dynamic_index_in_dim(stored, energy_slot, 0, keepdims=False)  44.3 us
    dynamic_update_slice x26, local copies, waits for them, and re-layouts, step(): stored = lax.dynamic_update_index_in_dim(stored, kept, energy_slot, 0)  34.2 us
    all_to_all x1, waiting for transfers between devices, per_device(): lax.all_to_all(paired, 'ch', split_axis=3, concat_axis=1, tiled=True)  31.9 us
    another operation x13, local copies, waits for them, and re-layouts  29.2 us
    convert_element_type x13, other arithmetic, step(): source = jnp.where(sector_index == 0, initial, incoming).astype(jnp.float32)  17.7 us
  transfers between devices with their start and end apart: 15, of which 13 were waited for; matrix products, arithmetic and copies ran while one was open for 11% of the time, Pallas kernels for 0%

commit v1 on v0

--- a/solution.py
+++ b/solution.py
@@ -1,6 +1,9 @@
+import functools
 import jax
 import jax.numpy as jnp
 from jax import lax
+from jax.experimental import pallas as pl
+from jax.experimental.pallas import tpu as pltpu
 from jax.sharding import PartitionSpec as P
 
 
@@ -10,7 +13,7 @@
     return lax.ppermute(value, axis, [(source, source + steps) for source in range(leading, last)])
 
 
-def per_device(start_amps, energies, thresholds, intersection):
+def per_device_pipelined(start_amps, energies, thresholds, intersection):
     sectors = lax.axis_size("sec")
     sector_index = lax.axis_index("sec")
     groups = lax.axis_size("ch")
@@ -67,6 +70,376 @@
     return returned.reshape(energy_count, row_count, width_cols)[None]
 
 
+AUX_ROWS = 16
+ROTATE_ROWS = 64
+
+
+def sweep_kernel(
+    sectors, groups, start, levels, own_block, out,
+    basis, amps, rotated, kept, turn,
+    local_sem, block_recv, spread_send, up_send, down_send, core_send,
+    start_recv, start_up, start_down, out_send, out_recv, out_local,
+):
+    k = lax.axis_index("sec")
+    z = lax.axis_index("ch")
+    core = k % 2
+    partner = k + 1 - 2 * core
+    pairs = sectors // 2
+    energy_count, row_count, width_cols = start.shape
+    half_cols = width_cols // 2
+    width = half_cols // sectors
+    channel_count = row_count * groups
+    has_up = z + 1 < groups
+    has_down = z >= 1
+
+    def remote(src, dst, send, recv, **where):
+        return pltpu.make_async_remote_copy(
+            src_ref=src, dst_ref=dst, send_sem=send, recv_sem=recv,
+            device_id=where, device_id_type=pl.DeviceIdType.MESH,
+        )
+
+    def rows_of(c):
+        return pl.ds(pl.multiple_of(c * row_count, row_count), row_count)
+
+    def block_up(i, c):
+        s = 2 * i + core
+        return remote(basis.at[s, c], basis.at[s, c], up_send.at[i, c], block_recv.at[s, c], ch=z + 1)
+
+    def block_down(i, c):
+        s = 2 * i + core
+        return remote(basis.at[s, c], basis.at[s, c], down_send.at[i, c], block_recv.at[s, c], ch=z - 1)
+
+    def block_core(i, c):
+        s = 2 * i + core
+        return remote(basis.at[s, c], basis.at[s, c], core_send.at[i, c], block_recv.at[s, c], sec=partner)
+
+    def block_spread(step):
+        target = 2 * ((k // 2 + step) % pairs) + core
+        return remote(basis.at[k, z], basis.at[k, z], spread_send.at[step], block_recv.at[k, z], sec=target)
+
+    def block_arrived(s, c):
+        remote(basis.at[s, c], basis.at[s, c], core_send.at[0, 0], block_recv.at[s, c], sec=partner).wait_recv()
+
+    def start_part(e, c):
+        return amps.at[0, e, rows_of(c), :]
+
+    def start_move(e, c, send, **where):
+        return remote(start_part(e, c), start_part(e, c), send.at[c], start_recv.at[e, c], **where)
+
+    def start_arrived(e, c):
+        remote(start_part(e, c), start_part(e, c), start_up.at[0], start_recv.at[e, c], sec=partner).wait_recv()
+
+    loads = [
+        pltpu.make_async_copy(own_block, basis.at[k, z], local_sem.at[0]),
+        pltpu.make_async_copy(
+            start.at[:, :, pl.ds(pl.multiple_of(k * width, width), width)],
+            amps.at[0, :, rows_of(z), pl.ds(0, width)], local_sem.at[1]),
+        pltpu.make_async_copy(
+            start.at[:, :, pl.ds(pl.multiple_of(half_cols + k * width, width), width)],
+            amps.at[0, :, rows_of(z), pl.ds(width, width)], local_sem.at[2]),
+    ]
+    for load in loads:
+        load.start()
+
+    barrier = pltpu.get_barrier_semaphore()
+    for step in range(1, sectors):
+        pl.semaphore_signal(barrier, inc=1, device_id={"sec": (k + step) % sectors}, device_id_type=pl.DeviceIdType.MESH)
+
+    @pl.when(has_up)
+    def _():
+        pl.semaphore_signal(barrier, inc=1, device_id={"ch": z + 1}, device_id_type=pl.DeviceIdType.MESH)
+
+    @pl.when(has_down)
+    def _():
+        pl.semaphore_signal(barrier, inc=1, device_id={"ch": z - 1}, device_id_type=pl.DeviceIdType.MESH)
+
+    line_peers = jnp.minimum(z, 1) + jnp.minimum(groups - 1 - z, 1)
+    pl.semaphore_wait(barrier, sectors - 1 + line_peers)
+    for load in loads:
+        load.wait()
+    for step in range(1, pairs):
+        block_spread(step).start()
+
+    def each_energy(action):
+        @pl.loop(0, energy_count)
+        def _(e):
+            action(e)
+
+    @pl.when(has_up)
+    def _():
+        each_energy(lambda e: start_move(e, z, start_up, ch=z + 1).start())
+
+    @pl.when(has_down)
+    def _():
+        each_energy(lambda e: start_move(e, z, start_down, ch=z - 1).start())
+
+    def own_step(i):
+        s = 2 * i + core
+
+        @pl.when(s != k)
+        def _():
+            block_arrived(s, z)
+
+        @pl.when(has_up)
+        def _():
+            block_up(i, z).start()
+
+        @pl.when(has_down)
+        def _():
+            block_down(i, z).start()
+
+        block_core(i, z).start()
+
+    def forward_step(i, d):
+        s = 2 * i + core
+
+        @pl.when(z - d >= 0)
+        def _():
+            block_arrived(s, z - d)
+
+            @pl.when(has_up)
+            def _():
+                block_up(i, z - d).start()
+
+            block_core(i, z - d).start()
+
+        @pl.when(z + d < groups)
+        def _():
+            block_arrived(s, z + d)
+
+            @pl.when(has_down)
+            def _():
+                block_down(i, z + d).start()
+
+            block_core(i, z + d).start()
+
+    def start_forward(d):
+        @pl.when(z - d >= 0)
+        def _():
+            def action(e):
+                start_arrived(e, z - d)
+
+                @pl.when(has_up)
+                def _():
+                    start_move(e, z - d, start_up, ch=z + 1).start()
+
+            each_energy(action)
+
+        @pl.when(z + d < groups)
+        def _():
+            def action(e):
+                start_arrived(e, z + d)
+
+                @pl.when(has_down)
+                def _():
+                    start_move(e, z + d, start_down, ch=z - 1).start()
+
+            each_energy(action)
+
+    own_step(0)
+    for d in range(1, groups):
+        start_forward(d)
+        forward_step(0, d)
+
+    def send_energy(s, e):
+        for half in range(2):
+            columns = pl.ds(pl.multiple_of(half * half_cols + k * width, width), width)
+
+            @pl.when(s == k)
+            def _():
+                pltpu.make_async_copy(kept.at[s, half, e], out.at[e, :, columns], out_local.at[0]).start()
+
+            @pl.when(s != k)
+            def _():
+                remote(kept.at[s, half, e], out.at[e, :, columns], out_send.at[s], out_recv.at[k], sec=s).start()
+
+    def rotate(s):
+        source = jnp.minimum(s, 1)
+
+        @pl.loop(0, groups)
+        def _(c):
+            limits = basis[s, c, row_count:, :row_count].astype(jnp.float32)[0:1, :]
+            wavenumber = jnp.sqrt(levels[...][:, 0:1] - limits)
+            cosine = jnp.cos(wavenumber)
+            sine_term = jnp.sin(wavenumber)
+            rows = wavenumber.shape[0]
+            filler = jnp.zeros((128 - 3 * rows, row_count), jnp.float32)
+            stacked = jnp.concatenate(
+                [cosine, sine_term / wavenumber, -wavenumber * sine_term, filler], axis=0
+            )
+            turn[...] = stacked.T
+
+            @pl.loop(0, row_count // ROTATE_ROWS)
+            def _(r):
+                local = pl.ds(pl.multiple_of(r * ROTATE_ROWS, ROTATE_ROWS), ROTATE_ROWS)
+                place = pl.ds(pl.multiple_of(c * row_count + r * ROTATE_ROWS, ROTATE_ROWS), ROTATE_ROWS)
+                factors = turn[local, :]
+                for e in range(energy_count):
+                    both = amps[source, e, place, :].astype(jnp.float32)
+                    values_part, slopes_part = both[:, :width], both[:, width:]
+                    keep = factors[:, e : e + 1]
+                    rise = factors[:, rows + e : rows + e + 1]
+                    fall = factors[:, 2 * rows + e : 2 * rows + e + 1]
+                    rotated[e, place, pl.ds(0, width)] = (keep * values_part + rise * slopes_part).astype(jnp.bfloat16)
+                    rotated[e, place, pl.ds(width, width)] = (fall * values_part + keep * slopes_part).astype(jnp.bfloat16)
+
+    def multiply(s):
+        @pl.loop(0, energy_count)
+        def _(e):
+            @pl.loop(0, groups)
+            def _(c):
+                @pl.when((s < sectors - 1) | (c == z))
+                def _():
+                    product = jnp.dot(
+                        basis[s, c, :row_count, :], rotated[e], preferred_element_type=jnp.float32
+                    ).astype(jnp.bfloat16)
+                    amps[1, e, rows_of(c), :] = product
+
+                    @pl.when(c == z)
+                    def _():
+                        kept[s, 0, e] = product[:, :width]
+                        kept[s, 1, e] = product[:, width:]
+
+            @pl.when(e >= 1)
+            def _():
+                send_energy(s, e - 1)
+
+    @pl.loop(0, pairs)
+    def _(i):
+        more = i + 1 < pairs
+
+        @pl.when(more)
+        def _():
+            own_step(i + 1)
+
+        for c in range(groups):
+            block_arrived(2 * i + 1 - core, c)
+        rotate(2 * i)
+
+        @pl.when(i >= 1)
+        def _():
+            send_energy(2 * i - 1, energy_count - 1)
+
+        multiply(2 * i)
+
+        @pl.when(more)
+        def _():
+            for d in range(1, groups - 1):
+                forward_step(i + 1, d)
+
+        rotate(2 * i + 1)
+        send_energy(2 * i, energy_count - 1)
+        multiply(2 * i + 1)
+
+        @pl.when(more)
+        def _():
+            forward_step(i + 1, groups - 1)
+
+    for step in range(1, pairs):
+        block_spread(step).wait_send()
+
+    @pl.loop(0, pairs)
+    def _(i):
+        for c in range(groups):
+            block_core(i, c).wait_send()
+
+            @pl.when(has_up & (c <= z))
+            def _():
+                block_up(i, c).wait_send()
+
+            @pl.when(has_down & (c >= z))
+            def _():
+                block_down(i, c).wait_send()
+
+    for c in range(groups):
+        span = amps.at[0, :, pl.ds(c * row_count, row_count), :]
+
+        @pl.when(has_up & (c <= z))
+        def _():
+            remote(span, span, start_up.at[c], start_recv.at[0, 0], ch=z + 1).wait_send()
+
+        @pl.when(has_down & (c >= z))
+        def _():
+            remote(span, span, start_down.at[c], start_recv.at[0, 0], ch=z - 1).wait_send()
+
+    send_energy(sectors - 1, energy_count - 1)
+
+    @pl.loop(0, sectors)
+    def _(s):
+        whole = remote(kept.at[s], kept.at[s], out_send.at[s], out_recv.at[s], sec=partner)
+
+        @pl.when(s != k)
+        def _():
+            whole.wait_send()
+            whole.wait_recv()
+
+        @pl.when(s == k)
+        def _():
+            pltpu.make_async_copy(kept.at[s], kept.at[s], out_local.at[0]).wait()
+
+
+def per_device_swept(start_amps, energies, thresholds, intersection):
+    sectors = lax.axis_size("sec")
+    groups = lax.axis_size("ch")
+    energy_count, row_count, width_cols = start_amps.shape
+    channel_count = intersection.shape[2]
+    width = width_cols // 2 // sectors
+    pairs = sectors // 2
+    padded = jnp.concatenate([energies, jnp.broadcast_to(energies[:1], (-energy_count % 8,))])
+    levels = jnp.broadcast_to(padded[:, None], (padded.shape[0], 128))
+    aux = jnp.pad(thresholds, ((0, AUX_ROWS - 1), (0, channel_count - row_count)))
+    own_block = jnp.concatenate([intersection[0], aux], axis=0)
+    dma = pltpu.SemaphoreType.DMA
+    stored = jax.ShapeDtypeStruct(start_amps.shape, jnp.bfloat16)
+    swept = pl.pallas_call(
+        functools.partial(sweep_kernel, sectors, groups),
+        out_shape=stored,
+        in_specs=[
+            pl.BlockSpec(memory_space=pl.ANY),
+            pl.BlockSpec(memory_space=pltpu.VMEM),
+            pl.BlockSpec(memory_space=pl.ANY),
+        ],
+        out_specs=pl.BlockSpec(memory_space=pl.ANY),
+        scratch_shapes=[
+            pltpu.VMEM((sectors, groups, row_count + AUX_ROWS, channel_count), jnp.bfloat16),
+            pltpu.VMEM((2, energy_count, channel_count, 2 * width), jnp.bfloat16),
+            pltpu.VMEM((energy_count, channel_count, 2 * width), jnp.bfloat16),
+            pltpu.VMEM((sectors, 2, energy_count, row_count, width), jnp.bfloat16),
+            pltpu.VMEM((row_count, 128), jnp.float32),
+            dma((3,)),
+            dma((sectors, groups)),
+            dma((pairs,)),
+            dma((pairs, groups)),
+            dma((pairs, groups)),
+            dma((pairs, groups)),
+            dma((energy_count, groups)),
+            dma((groups,)),
+            dma((groups,)),
+            dma((sectors,)),
+            dma((sectors,)),
+            dma((1,)),
+        ],
+        compiler_params=pltpu.CompilerParams(
+            collective_id=0, has_side_effects=True, vmem_limit_bytes=60 * 2**20
+        ),
+    )(start_amps, levels, own_block)
+    return swept[None]
+
+
+GATHERED_LIMIT = 24 * 2**20
+
+
+def per_device(start_amps, energies, thresholds, intersection):
+    sectors = lax.axis_size("sec")
+    row_count, channel_count = intersection.shape[1:]
+    gathered_bytes = sectors * channel_count**2 * intersection.dtype.itemsize
+    even = sectors % 2 == 0 and (start_amps.shape[2] // 2) % (sectors * 128) == 0
+    even = even and row_count % 128 == 0 and energies.shape[0] <= 40
+    if even and gathered_bytes <= GATHERED_LIMIT:
+        return per_device_swept(start_amps, energies, thresholds, intersection)
+    return per_device_pipelined(start_amps, energies, thresholds, intersection)
+
+
 def solution(mesh):
     in_specs = (P(None, "ch", None), P(), P("sec", "ch"), P("sec", "ch", None))
     out_specs = P("sec", None, "ch", None)

time: 746 us -> 295 us (0.40); the launches traced: 733 us -> 295 us
  Pallas kernels: 0 us -> 285 us
  blocking collectives: 279 us -> 0 us
  local copies, waits for them, and re-layouts: 206 us -> 8.58 us
  waiting for transfers between devices: 160 us -> 0 us
  other arithmetic: 38.1 us -> 1.9 us
  starting transfers between devices: 22.1 us -> 0 us
  matrix products: 13.9 us -> 0 us
  between operations: 13.4 us -> 0.01 us
    pallas_call x0 -> x1, Pallas kernels: none -> 285 us  [per_device_swept(): pl.pallas_call(functools.partial(sweep_kernel, sectors, groups), out_shap...]
    all_to_all x1 -> x0, blocking collectives: 140 us -> none  [per_device(): lax.all_to_all(final_pair[1], 'ch', split_axis=1, concat_axis=3, tiled=True)]
    all_gather x1 -> x0, blocking collectives: 139 us -> none  [per_device(): lax.all_gather(thresholds, 'ch', axis=1, tiled=True)]
    ppermute x13 -> x0, waiting for transfers between devices: 127 us -> none  [passed_along(): lax.ppermute(value, axis, [(source, source + steps) for source in range(l...]
    dynamic_slice x39 -> x0, local copies, waits for them, and re-layouts: 52.9 us -> none  [the longest x26 44.3 us: step(): previous = lax.dynamic_index_in_dim(stored, energy_slot, 0, keepdims=False)]
    another operation x14 -> x0, local copies, waits for them, and re-layouts: 40.3 us -> none
    dynamic_update_slice x26 -> x0, local copies, waits for them, and re-layouts: 34.2 us -> none  [step(): stored = lax.dynamic_update_index_in_dim(stored, kept, energy_slot, 0)]
    all_to_all x1 -> x0, waiting for transfers between devices: 31.9 us -> none  [per_device(): lax.all_to_all(paired, 'ch', split_axis=3, concat_axis=1, tiled=True)]
  transfers between devices with their start and end apart: 15 -> 0, of which waited for: 13 -> 0; matrix products, arithmetic and copies ran while one was open for 11% -> 0% of each run, Pallas kernels for 0% -> 0%
where the time goes in v1:
time: 295 us
  Pallas kernels  285 us (97%)
  local copies, waits for them, and re-layouts  8.58 us (3%)
    pallas_call x1, Pallas kernels, per_device_swept(): pl.pallas_call(functools.partial(sweep_kernel, sectors, groups), out_shap...  285 us
    unnamed x1, local copies, waits for them, and re-layouts  6.61 us

profile of v1, /device:TPU:7, one launch (start us, length us, event | category | flops | bytes accessed | tf_op | source)
XLA Modules:
  0.0 295.0 jit_solution(9426091673744717324)
XLA Ops:
  0.0 1.3 concatenate.6
  1.3 0.7 broadcast_in_dim.7.levels
  2.0 1.9 fusion.1.own_block
  3.9 284.5 %shard_map.46 = bf16[6,256,2048]{2,1,0:T(8,128)(2,1)} custom-call(bf16[6,256,2048]{2,1,0:T(8,128)(2,1)} %start.1, f32[8,128]{1,0:T(8,128)} %broadcast_in_dim.7.levels, bf16[272,1024]{1,0:T(8,128)(2,1)} %fusion.1.own_block), custom_call_target="tpu_custom_call" | custom-call | tf_op jit(solution)/shard_map/pallas_call | solution.py:394
  288.4 6.6 %copy.6 = bf16[1,6,256,2048]{3,2,1,0:T(8,128)(2,1)} copy(bf16[1,6,256,2048]{3,2,1,0:T(8,128)(2,1)} %bitcast.4) | data formatting | bytes 12582912

commit v2 on v1

--- a/solution.py
+++ b/solution.py
@@ -236,10 +236,15 @@
 
             each_energy(action)
 
+    lag = max(groups // 2, 1)
     own_step(0)
     for d in range(1, groups):
         start_forward(d)
         forward_step(0, d)
+        if pairs > 1 and d == lag:
+            own_step(1)
+        if pairs > 1 and d > lag:
+            forward_step(1, d - lag)
 
     def send_energy(s, e):
         for half in range(2):
@@ -307,10 +312,11 @@
     @pl.loop(0, pairs)
     def _(i):
         more = i + 1 < pairs
-
-        @pl.when(more)
-        def _():
-            own_step(i + 1)
+        further = i + 2 < pairs
+
+        @pl.when(further)
+        def _():
+            own_step(i + 2)
 
         for c in range(groups):
             block_arrived(2 * i + 1 - core, c)
@@ -324,7 +330,7 @@
 
         @pl.when(more)
         def _():
-            for d in range(1, groups - 1):
+            for d in range(max(groups - lag, 1), groups - 1):
                 forward_step(i + 1, d)
 
         rotate(2 * i + 1)
@@ -334,6 +340,11 @@
         @pl.when(more)
         def _():
             forward_step(i + 1, groups - 1)
+
+        @pl.when(further)
+        def _():
+            for d in range(1, groups - lag):
+                forward_step(i + 2, d)
 
     for step in range(1, pairs):
         block_spread(step).wait_send()

time: 295 us -> 291 us (0.986)
  Pallas kernels: 285 us -> 280 us
    pallas_call x1, Pallas kernels: 285 us -> 280 us  [per_device_swept(): pl.pallas_call(functools.partial(sweep_kernel, sectors, groups), out_shap...]
where the time goes in v2:
time: 291 us
  Pallas kernels  280 us (96%)
  local copies, waits for them, and re-layouts  8.58 us (3%)
    pallas_call x1, Pallas kernels, per_device_swept(): pl.pallas_call(functools.partial(sweep_kernel, sectors, groups), out_shap...  280 us
    unnamed x1, local copies, waits for them, and re-layouts  6.61 us

profile of v2, /device:TPU:7, one launch (start us, length us, event | category | flops | bytes accessed | tf_op | source)
XLA Modules:
  0.0 291.0 jit_solution(6475032391501084918)
XLA Ops:
  0.0 1.3 concatenate.6
  1.3 0.7 broadcast_in_dim.7.levels
  2.0 1.9 fusion.1.own_block
  3.9 280.5 %shard_map.46 = bf16[6,256,2048]{2,1,0:T(8,128)(2,1)} custom-call(bf16[6,256,2048]{2,1,0:T(8,128)(2,1)} %start.1, f32[8,128]{1,0:T(8,128)} %broadcast_in_dim.7.levels, bf16[272,1024]{1,0:T(8,128)(2,1)} %fusion.1.own_block), custom_call_target="tpu_custom_call" | custom-call | tf_op jit(solution)/shard_map/pallas_call | solution.py:405
  284.3 6.6 %copy.6 = bf16[1,6,256,2048]{3,2,1,0:T(8,128)(2,1)} copy(bf16[1,6,256,2048]{3,2,1,0:T(8,128)(2,1)} %bitcast.4) | data formatting | bytes 12582912

commit v3 on v2

--- a/solution.py
+++ b/solution.py
@@ -237,12 +237,13 @@
             each_energy(action)
 
     lag = max(groups // 2, 1)
-    own_step(0)
+    for i in range(min(pairs, 2)):
+        own_step(i)
     for d in range(1, groups):
         start_forward(d)
         forward_step(0, d)
-        if pairs > 1 and d == lag:
-            own_step(1)
+        if pairs > 2 and d == 1:
+            own_step(2)
         if pairs > 1 and d > lag:
             forward_step(1, d - lag)
 
@@ -314,9 +315,9 @@
         more = i + 1 < pairs
         further = i + 2 < pairs
 
-        @pl.when(further)
-        def _():
-            own_step(i + 2)
+        @pl.when(i + 3 < pairs)
+        def _():
+            own_step(i + 3)
 
         for c in range(groups):
             block_arrived(2 * i + 1 - core, c)

time: 291 us -> 295 us (1.014)
  Pallas kernels: 280 us -> 284 us
    pallas_call x1, Pallas kernels: 280 us -> 284 us  [per_device_swept(): pl.pallas_call(functools.partial(sweep_kernel, sectors, groups), out_shap...]
where the time goes in v3:
time: 295 us
  Pallas kernels  284 us (96%)
  local copies, waits for them, and re-layouts  8.58 us (3%)
    pallas_call x1, Pallas kernels, per_device_swept(): pl.pallas_call(functools.partial(sweep_kernel, sectors, groups), out_shap...  284 us
    unnamed x1, local copies, waits for them, and re-layouts  6.61 us

profile of v3, /device:TPU:7, one launch (start us, length us, event | category | flops | bytes accessed | tf_op | source)
XLA Modules:
  0.0 294.5 jit_solution(18446438923066294071)
XLA Ops:
  0.0 1.3 concatenate.6
  1.3 0.7 broadcast_in_dim.7.levels
  2.0 1.9 fusion.1.own_block
  3.9 284.0 %shard_map.46 = bf16[6,256,2048]{2,1,0:T(8,128)(2,1)} custom-call(bf16[6,256,2048]{2,1,0:T(8,128)(2,1)} %start.1, f32[8,128]{1,0:T(8,128)} %broadcast_in_dim.7.levels, bf16[272,1024]{1,0:T(8,128)(2,1)} %fusion.1.own_block), custom_call_target="tpu_custom_call" | custom-call | tf_op jit(solution)/shard_map/pallas_call | solution.py:406
  287.9 6.6 %copy.6 = bf16[1,6,256,2048]{3,2,1,0:T(8,128)(2,1)} copy(bf16[1,6,256,2048]{3,2,1,0:T(8,128)(2,1)} %bitcast.4) | data formatting | bytes 12582912
